TPU v7x, 32 devices: a whole 2x2x4 slice. The times are simulated.
32 devices in a mesh: dp: 8 (over z, y), seq: 4 (over x, core).
Axes of the slice: x: 2, y: 2, z: 4, core: 2. Of those that a mesh axis runs over, the one named last changes fastest.
Arguments:
- tokens: bfloat16 [16, 2048, 768], P('dp', 'seq'), may hold values from -6 to 6
- first_values: bfloat16 [16, 2048, 384], P('dp', 'seq'), may hold values from -6 to 6
- cotangent: bfloat16 [16, 2048, 768], P('dp', 'seq'), may hold values from -6 to 6
- lengths: int32 [16], P('dp'), may hold values from 64 to 2048, as said below
- master_tiles: float32 [416, 128, 128], P(('dp', 'seq'))
- left_stat: float32 [416, 128, 128], P(('dp', 'seq'))
- right_stat: float32 [416, 128, 128], P(('dp', 'seq'))
- left_root: float32 [416, 128, 128], P(('dp', 'seq'))
- right_root: float32 [416, 128, 128], P(('dp', 'seq'))
- vector_params: float32 [8832], replicated
- vector_stat: float32 [8832], replicated
Outputs:
- block_output: bfloat16 [16, 2048, 768], P('dp', 'seq')
- tokens_grad: float32 [16, 2048, 768], P('dp', 'seq')
- first_values_grad: float32 [16, 2048, 384], P('dp', 'seq')
- tile_grads: float32 [416, 128, 128], P(('dp', 'seq'))
- left_new: float32 [416, 128, 128], P(('dp', 'seq'))
- right_new: float32 [416, 128, 128], P(('dp', 'seq'))
- tiles_new: float32 [416, 128, 128], P(('dp', 'seq'))
- vector_grads: float32 [8832], replicated
- vector_stat_new: float32 [8832], replicated
- vector_new: float32 [8832], replicated
- grad_norm: float32 [], replicated
Inputs may be any that keep to these rules, and one draw needn't show every extreme that they name: `lengths`: each sequence's length; in every draw some sequence has exactly 2048.
All inputs are finite; a program needn't handle non-finite values.
Results may differ from a plain program's by a relative error of at most 0.012.
The roundings to bfloat16 on the way count: a program that leaves them out, or rounds other values in their place, can miss the bound.
Values may be sent and summed in bfloat16 or wider, within the bound.
A program may use at most 192 MiB of HBM per device.

v0:
```python
import jax
import jax.numpy as jnp
from jax import lax
from jax.sharding import PartitionSpec as P

D = 768
HD = 64
FF = 3072
VW = 384
QBLK = 512
TILE = 128
CLIP = 256
highest = lax.Precision.HIGHEST
norm_eps = 1e-05
clip_eps = 1e-06
decay_rate = 0.5
matrix_rate = 0.3
vector_rate = 0.1
moment_eps = 1e-08
masked_score = -1e30


def matrix_shapes():
    return ((D, D), (D, D), (D, VW), (D, D), (D, FF), (FF, D))


def untile(stacked, row_count, col_count):
    shaped = stacked.reshape(row_count // TILE, col_count // TILE, TILE, TILE)
    return shaped.transpose(0, 2, 1, 3).reshape(row_count, col_count)


def retile(matrix):
    row_count, col_count = matrix.shape
    shaped = matrix.reshape(row_count // TILE, TILE, col_count // TILE, TILE)
    return shaped.transpose(0, 2, 1, 3).reshape(-1, TILE, TILE)


def split_tiles(stacked):
    matrices = []
    offset = 0
    for row_count, col_count in matrix_shapes():
        amount = row_count // TILE * (col_count // TILE)
        matrices.append(untile(stacked[offset : offset + amount], row_count, col_count))
        offset = offset + amount
    return matrices


def join_tiles(matrices, total_tiles):
    joined = jnp.concatenate([retile(matrix) for matrix in matrices], axis=0)
    padding = jnp.zeros((total_tiles - joined.shape[0], TILE, TILE), joined.dtype)
    return jnp.concatenate([joined, padding], axis=0)


def split_vector(vector):
    pieces = []
    offset = 0
    for length in (D, D, D, D, D, D, D, VW, FF):
        pieces.append(vector[offset : offset + length])
        offset = offset + length
    return pieces


def matmul(left_in, right_in):
    return jnp.dot(left_in, right_in, preferred_element_type=jnp.float32)


def contract_rows(left_in, right_in):
    return lax.dot_general(
        left_in, right_in, (((0,), (0,)), ((), ())), preferred_element_type=jnp.float32
    )


def contract_cols(left_in, right_in):
    return lax.dot_general(
        left_in, right_in, (((1,), (1,)), ((), ())), preferred_element_type=jnp.float32
    )


def norm_forward(values, gain_row, shift_row):
    centered = values - jnp.mean(values, axis=-1, keepdims=True)
    variance = jnp.mean(centered * centered, axis=-1, keepdims=True)
    inv_std = lax.rsqrt(variance + norm_eps)
    unit_rows = centered * inv_std
    return (unit_rows * gain_row + shift_row, unit_rows, inv_std)


def norm_backward(grad_in, unit_rows, inv_std, gain_row):
    scaled = grad_in * gain_row
    term = (
        scaled
        - jnp.mean(scaled, axis=-1, keepdims=True)
        - unit_rows * jnp.mean(scaled * unit_rows, axis=-1, keepdims=True)
    )
    return (term * inv_std, jnp.sum(grad_in * unit_rows, axis=0), jnp.sum(grad_in, axis=0))


def allowed_keys(block_index, length, key_count):
    query_pos = block_index * QBLK + jnp.arange(QBLK, dtype=jnp.int32)
    key_pos = jnp.arange(key_count, dtype=jnp.int32)
    return (key_pos[None, :] <= query_pos[:, None]) & (key_pos[None, :] < length)


def attend_forward(inputs):
    query_seq, key_seq, value_seq, length = inputs
    key_count = query_seq.shape[0]
    head_count = query_seq.shape[1] // HD
    query_heads = query_seq.reshape(key_count, head_count, HD)
    key_heads = key_seq.reshape(key_count, head_count, HD)
    value_heads = value_seq.reshape(key_count, head_count, HD)
    score_scale = HD ** (-0.5)

    def one_block(block_index):
        query_rows = lax.dynamic_slice_in_dim(query_heads, block_index * QBLK, QBLK, 0)
        scores = (
            jnp.einsum("qhd,khd->hqk", query_rows, key_heads, preferred_element_type=jnp.float32)
            * score_scale
        )
        scores = jnp.where(allowed_keys(block_index, length, key_count)[None], scores, masked_score)
        top_score = jnp.max(scores, axis=-1, keepdims=True)
        exponent = jnp.exp(scores - top_score)
        totals = jnp.sum(exponent, axis=-1, keepdims=True)
        weights = (exponent / totals).astype(jnp.bfloat16)
        attended = jnp.einsum(
            "hqk,khd->qhd", weights, value_heads, preferred_element_type=jnp.float32
        )
        return (attended.astype(jnp.bfloat16), (top_score + jnp.log(totals))[..., 0])

    attended, log_sums = lax.map(one_block, jnp.arange(key_count // QBLK, dtype=jnp.int32))
    return (
        attended.reshape(key_count, head_count * HD),
        log_sums.transpose(1, 0, 2).reshape(head_count, key_count),
    )


def attend_backward(inputs):
    query_seq, key_seq, value_seq, grad_seq, log_sums, length = inputs
    key_count = query_seq.shape[0]
    head_count = query_seq.shape[1] // HD
    query_heads = query_seq.reshape(key_count, head_count, HD)
    key_heads = key_seq.reshape(key_count, head_count, HD)
    value_heads = value_seq.reshape(key_count, head_count, HD)
    grad_heads = grad_seq.reshape(key_count, head_count, HD)
    score_scale = HD ** (-0.5)

    def one_block(carried, block_index):
        key_acc, value_acc = carried
        query_rows = lax.dynamic_slice_in_dim(query_heads, block_index * QBLK, QBLK, 0)
        grad_rows = lax.dynamic_slice_in_dim(grad_heads, block_index * QBLK, QBLK, 0)
        sums_rows = lax.dynamic_slice_in_dim(log_sums, block_index * QBLK, QBLK, 1)
        scores = (
            jnp.einsum("qhd,khd->hqk", query_rows, key_heads, preferred_element_type=jnp.float32)
            * score_scale
        )
        scores = jnp.where(allowed_keys(block_index, length, key_count)[None], scores, masked_score)
        probs = jnp.exp(scores - sums_rows[..., None])
        probs_grad = jnp.einsum(
            "qhd,khd->hqk", grad_rows, value_heads, preferred_element_type=jnp.float32
        )
        delta = jnp.sum(probs * probs_grad, axis=-1, keepdims=True)
        score_grad = (probs * (probs_grad - delta)).astype(jnp.bfloat16)
        query_grad = (
            jnp.einsum("hqk,khd->qhd", score_grad, key_heads, preferred_element_type=jnp.float32)
            * score_scale
        )
        key_acc = (
            key_acc
            + jnp.einsum("hqk,qhd->khd", score_grad, query_rows, preferred_element_type=jnp.float32)
            * score_scale
        )
        value_acc = value_acc + jnp.einsum(
            "hqk,qhd->khd",
            probs.astype(jnp.bfloat16),
            grad_rows,
            preferred_element_type=jnp.float32,
        )
        return ((key_acc, value_acc), query_grad.astype(jnp.bfloat16))

    zero_acc = jnp.zeros((key_count, head_count, HD), jnp.float32)
    (key_acc, value_acc), query_grad = lax.scan(
        one_block, (zero_acc, zero_acc), jnp.arange(key_count // QBLK, dtype=jnp.int32)
    )
    local_width = head_count * HD
    return (
        query_grad.reshape(key_count, local_width),
        key_acc.astype(jnp.bfloat16).reshape(key_count, local_width),
        value_acc.astype(jnp.bfloat16).reshape(key_count, local_width),
    )


def per_device(
    tokens,
    first_values,
    cotangent,
    lengths,
    master_tiles,
    left_stat,
    right_stat,
    left_root,
    right_root,
    vector_params,
    vector_stat,
):
    seq_count, block_len, model_width = tokens.shape
    gathered = lax.all_gather(master_tiles.astype(jnp.bfloat16), ("dp", "seq"), axis=0, tiled=True)
    w_query, w_key, w_value, w_out, w_hidden, w_proj = split_tiles(gathered)
    (
        gain_one,
        shift_one,
        gain_two,
        shift_two,
        query_bias,
        out_bias,
        proj_bias,
        value_bias,
        hidden_bias,
    ) = split_vector(vector_params)
    flat_tokens = tokens.reshape(-1, model_width).astype(jnp.float32)
    normed_one, unit_one, inv_one = norm_forward(flat_tokens, gain_one, shift_one)
    normed_one = normed_one.astype(jnp.bfloat16)
    queries = (matmul(normed_one, w_query) + query_bias).astype(jnp.bfloat16)
    keys_all = matmul(normed_one, w_key).astype(jnp.bfloat16)
    fresh = (matmul(normed_one, w_value) + value_bias).astype(jnp.bfloat16)
    values_all = jnp.concatenate([fresh, first_values.reshape(-1, VW)], axis=-1)
    packed = jnp.stack([queries, keys_all, values_all]).reshape(
        3, seq_count, block_len, model_width
    )
    head_data = lax.all_to_all(packed, "seq", split_axis=3, concat_axis=2, tiled=True)
    attn_heads, log_sums = lax.map(
        attend_forward, (head_data[0], head_data[1], head_data[2], lengths)
    )
    returned = lax.all_to_all(attn_heads, "seq", split_axis=1, concat_axis=2, tiled=True)
    attended = returned.reshape(-1, model_width)
    residual = flat_tokens + matmul(attended, w_out) + out_bias
    normed_two, unit_two, inv_two = norm_forward(residual, gain_two, shift_two)
    normed_two = normed_two.astype(jnp.bfloat16)
    hidden = matmul(normed_two, w_hidden) + hidden_bias
    active = jax.nn.gelu(hidden, approximate=True).astype(jnp.bfloat16)
    output = residual + matmul(active, w_proj) + proj_bias
    block_output = output.astype(jnp.bfloat16).reshape(tokens.shape)
    positions = lax.axis_index("seq") * block_len + jnp.arange(block_len, dtype=jnp.int32)
    live = positions[None, :] < lengths[:, None]
    out_grad = jnp.where(live[:, :, None], cotangent, jnp.zeros_like(cotangent)).reshape(
        -1, model_width
    )
    grad_w_proj = contract_rows(active, out_grad)
    proj_bias_grad = jnp.sum(out_grad.astype(jnp.float32), axis=0)
    active_grad = contract_cols(out_grad, w_proj)
    gelu_value, gelu_back = jax.vjp(lambda inner: jax.nn.gelu(inner, approximate=True), hidden)
    hidden_grad = gelu_back(active_grad)[0].astype(jnp.bfloat16)
    grad_w_hidden = contract_rows(normed_two, hidden_grad)
    hidden_bias_grad = jnp.sum(hidden_grad.astype(jnp.float32), axis=0)
    norm_two_in = contract_cols(hidden_grad, w_hidden)
    resid_part, gain_two_grad, shift_two_grad = norm_backward(
        norm_two_in, unit_two, inv_two, gain_two
    )
    residual_grad = out_grad.astype(jnp.float32) + resid_part
    branch_grad = residual_grad.astype(jnp.bfloat16)
    grad_w_out = contract_rows(attended, branch_grad)
    out_bias_grad = jnp.sum(branch_grad.astype(jnp.float32), axis=0)
    attended_grad = contract_cols(branch_grad, w_out).astype(jnp.bfloat16)
    grad_heads = lax.all_to_all(
        attended_grad.reshape(seq_count, block_len, model_width),
        "seq",
        split_axis=2,
        concat_axis=1,
        tiled=True,
    )
    query_grad, key_grad, value_grad = lax.map(
        attend_backward, (head_data[0], head_data[1], head_data[2], grad_heads, log_sums, lengths)
    )
    sent_back = lax.all_to_all(
        jnp.stack([query_grad, key_grad, value_grad]),
        "seq",
        split_axis=2,
        concat_axis=3,
        tiled=True,
    )
    queries_grad = sent_back[0].reshape(-1, model_width)
    keys_grad = sent_back[1].reshape(-1, model_width)
    values_grad = sent_back[2].reshape(-1, model_width)
    fresh_grad = values_grad[:, :VW]
    first_grad = values_grad[:, VW:].astype(jnp.float32).reshape(first_values.shape)
    grad_w_query = contract_rows(normed_one, queries_grad)
    grad_w_key = contract_rows(normed_one, keys_grad)
    grad_w_value = contract_rows(normed_one, fresh_grad)
    query_bias_grad = jnp.sum(queries_grad.astype(jnp.float32), axis=0)
    value_bias_grad = jnp.sum(fresh_grad.astype(jnp.float32), axis=0)
    norm_one_in = (
        contract_cols(queries_grad, w_query)
        + contract_cols(keys_grad, w_key)
        + contract_cols(fresh_grad, w_value)
    )
    token_part, gain_one_grad, shift_one_grad = norm_backward(
        norm_one_in, unit_one, inv_one, gain_one
    )
    tokens_grad = (residual_grad + token_part).reshape(tokens.shape)
    grad_stack = join_tiles(
        [grad_w_query, grad_w_key, grad_w_value, grad_w_out, grad_w_hidden, grad_w_proj],
        gathered.shape[0],
    )
    vector_local = jnp.concatenate(
        [
            gain_one_grad,
            shift_one_grad,
            gain_two_grad,
            shift_two_grad,
            query_bias_grad,
            out_bias_grad,
            proj_bias_grad,
            value_bias_grad,
            hidden_bias_grad,
        ]
    )
    owned = lax.psum_scatter(grad_stack, ("dp", "seq"), scatter_dimension=0, tiled=True)
    summed_vector, owned_square = lax.psum((vector_local, jnp.sum(owned * owned)), ("dp", "seq"))
    grad_norm = jnp.sqrt(owned_square + jnp.sum(summed_vector * summed_vector))
    factor = jnp.minimum(1.0, CLIP / (grad_norm + clip_eps))
    clipped = owned * factor
    left_gram = jnp.einsum("tij,tkj->tik", clipped, clipped, precision=highest)
    right_gram = jnp.einsum("tji,tjk->tik", clipped, clipped, precision=highest)
    inner = jnp.einsum("tij,tjk->tik", clipped, right_root, precision=highest)
    step = jnp.einsum("tij,tjk->tik", left_root, inner, precision=highest)
    left_new = decay_rate * left_stat + (1.0 - decay_rate) * left_gram
    right_new = decay_rate * right_stat + (1.0 - decay_rate) * right_gram
    tiles_new = master_tiles - matrix_rate * step
    vector_grads = summed_vector * factor
    vector_stat_new = decay_rate * vector_stat + (1.0 - decay_rate) * vector_grads * vector_grads
    vector_new = vector_params - vector_rate * vector_grads / (
        jnp.sqrt(vector_stat_new) + moment_eps
    )
    return (
        block_output,
        tokens_grad,
        first_grad,
        clipped,
        left_new,
        right_new,
        tiles_new,
        vector_grads,
        vector_stat_new,
        vector_new,
        grad_norm,
    )


def solution(mesh):
    in_specs = (
        P("dp", "seq", None),
        P("dp", "seq", None),
        P("dp", "seq", None),
        P("dp"),
        P(("dp", "seq"), None, None),
        P(("dp", "seq"), None, None),
        P(("dp", "seq"), None, None),
        P(("dp", "seq"), None, None),
        P(("dp", "seq"), None, None),
        P(),
        P(),
    )
    out_specs = (
        P("dp", "seq", None),
        P("dp", "seq", None),
        P("dp", "seq", None),
        P(("dp", "seq"), None, None),
        P(("dp", "seq"), None, None),
        P(("dp", "seq"), None, None),
        P(("dp", "seq"), None, None),
        P(),
        P(),
        P(),
        P(),
    )
    return jax.shard_map(
        per_device, mesh=mesh, in_specs=in_specs, out_specs=out_specs, check_vma=False
    )
```

profile of v0, /device:TPU:0, one launch (start us, length us, event | category | flops | bytes accessed | tf_op | source)
XLA Modules:
  0.0 1392.7 jit_solution(12912429408049028219)
XLA Ops:
  17.5 97.4 %all-gather.2.cloned.1.call-done = bf16[416,128,128]{2,1,0:T(8,128)(2,1)} async-done(((bf16[13,128,128]{2,1,0:T(8,128)(2,1)}), bf16[416,128,128]{2,1,0:T(8,128)(2,1)}) %all-gather.2.cloned.1.call-update) | async-done | bytes 13631504 | tf_op jit(solution)/shard_map/all_gather | solution.py:204
  143.5 13.7 maximum_maximum_fusion
  163.1 53.2 %all-to-all-done = bf16[3,2,512,768]{2,1,0,3:T(2,128)(2,1)} async-done(((bf16[3,2,512,768]{2,1,0,3:T(2,128)(2,1)}), bf16[3,2,512,768]{2,1,0,3:T(2,128)(2,1)}, u32[]{:S(2)}, u32[]{:S(2)}) %all-to-all-start) | async-done | bytes 4718624 | tf_op jit(solution)/shard_map/all_to_all | solution.py:227
  242.3 197.6 %while.54 = (s32[]{:T(128)}, bf16[2,2048,192]{1,2,0:T(8,128)(2,1)}, f32[2,3,2048]{2,1,0:T(4,128)S(1)}, bf16[2,2048,192]{1,2,0:T(8,128)(2,1)}, bf16[2,2048,192]{1...) while((s32[]{:T(128)}, bf16[2,2048,192]{1,2,0:T(8,128)(2,1)}, ...), condition=%wide.region_7.8_spmd, body=%wide.region_2.7_spmd.sunk | while | flops 845251584 | bytes 53479908 | solution.py:228
  246.7 92.3 %while.57 = (s32[]{:T(128)}, bf16[4,512,3,64]{1,3,2,0:T(8,128)(2,1)S(1)}, f32[4,3,512]{2,1,0:T(4,128)S(1)}, s32[4]{0:T(128)S(1)}, s32[]{:T(128)}, /*index=5*/bf1...) while((s32[]{:T(128)}, ...), condition=%wide.region_6.6_spmd, body=%wide.region_3.5_spmd.sunk | while | flops 845251584 | bytes 43976908 | solution.py:128
  249.2 7.0 fusion.206
  256.2 6.8 fusion.207
  263.0 6.7 fusion.208
  272.3 7.0 fusion.206
  279.3 6.8 fusion.207
  286.1 6.7 fusion.208
  295.4 7.0 fusion.206
  302.4 6.8 fusion.207
  309.2 6.7 fusion.208
  318.5 7.0 fusion.206
  325.5 6.8 fusion.207
  332.3 6.7 fusion.208
  345.3 92.3 %while.57 = (s32[]{:T(128)}, bf16[4,512,3,64]{1,3,2,0:T(8,128)(2,1)S(1)}, f32[4,3,512]{2,1,0:T(4,128)S(1)}, s32[4]{0:T(128)S(1)}, s32[]{:T(128)}, /*index=5*/bf1...) while((s32[]{:T(128)}, ...), condition=%wide.region_6.6_spmd, body=%wide.region_3.5_spmd.sunk | while | flops 845251584 | bytes 43976908 | solution.py:128
  347.9 7.0 fusion.206
  354.9 6.8 fusion.207
  361.7 6.7 fusion.208
  371.0 7.0 fusion.206
  378.0 6.8 fusion.207
  384.8 6.7 fusion.208
  394.1 7.0 fusion.206
  401.1 6.8 fusion.207
  417.2 7.0 fusion.206
  424.2 6.8 fusion.207
  431.0 6.7 fusion.208
  453.6 9.1 fusion.122
  467.8 6.9 copy.229
  479.3 10.4 copy.226
  495.2 22.7 %fusion.54 = (bf16[3072,1024]{0,1:T(8,128)(2,1)}, f32[1024,3072]{1,0:T(8,128)}) fusion(f32[3072]{0:T(1024)S(1)} %copy-done.64, bf16[96,8,24,128]{3,2,1,0:T(8,128)(2,1)S(1)} %bitcast.413, f32[1024,768]{1,0:T(8,128)S(1)} %get-tuple-element.458, f32[768]{0:T(1024)S(1)} %copy-done.51, f32[768]{0:T(1024)S(1)} %copy-done.49, f32[1024]{0:T(1024)S(1)} %add_rsqrt_fusion, ...), kind=kOutput, calls=%fused_computation.81 | convolution fusion | flops 4867227648 | bytes 26765312 | tf_op jit(solution)/shard_map/dot_general | solution.py:64
  517.9 15.1 %convert_reduce_fusion = (f32[3072]{0:T(1024)}, bf16[1024,3072]{1,0:T(8,128)(2,1)S(1)}) fusion(f32[1024,3072]{1,0:T(8,128)} %get-tuple-element.462, f32[3072]{0:T(1024)S(1)} %copy-done.64, bf16[1024,768]{1,0:T(8,128)(2,1)S(1)} %bitcast.391, bf16[96,8,24,128]{3,2,1,0:T(8,128)(2,1)S(1)} %bitcast.410), kind=kOutput, calls=%fused_computation.82 | convolution fusion | flops 4904186880 | bytes 25190400 | tf_op jit(solution)/shard_map/dot_general | solution.py:74
  556.1 8.6 copy.261
  564.7 8.7 all-to-all-done.2
  579.3 277.4 %while.56 = (s32[]{:T(128)}, bf16[2,2048,192]{1,2,0:T(8,128)(2,1)}, bf16[2,2048,192]{1,2,0:T(8,128)(2,1)}, bf16[2,2048,192]{1,2,0:T(8,128)(2,1)}, bf16[2,2048,19...) while((s32[]{:T(128)}, bf16[2,2048,192]{1,2,0:T(8,128)(2,1)}, ...), condition=%wide.region_16.17_spmd, body=%wide.region_12.16_spmd.sunk | while | flops 2065499136 | bytes 171613168 | solution.py:268
  586.7 121.9 %while.58 = (s32[]{:T(128)}, f32[2048,3,64]{0,2,1:T(8,128)S(1)}, f32[2048,3,64]{0,2,1:T(8,128)}, bf16[4,512,3,64]{1,3,2,0:T(8,128)(2,1)}, s32[4]{0:T(128)S(1)}, ...) while((s32[]{:T(128)}, f32[2048,3,64]{0,2,1:T(8,128)S(1)}, ...), condition=%wide.region_15.15_spmd.clone, body=%wide.region_13.14_spmd.clone.sunk | while | flops 2064712704 | bytes 114546992 | solution.py:179
  597.1 7.1 multiply_reduce_fusion.9
  604.2 6.9 multiply_convert_fusion.6
  627.9 7.1 multiply_reduce_fusion.9
  635.1 6.9 multiply_convert_fusion.6
  658.8 7.1 multiply_reduce_fusion.9
  665.9 6.9 multiply_convert_fusion.6
  689.6 7.1 multiply_reduce_fusion.9
  696.8 6.9 multiply_convert_fusion.6
  725.1 121.9 %while.58 = (s32[]{:T(128)}, f32[2048,3,64]{0,2,1:T(8,128)S(1)}, f32[2048,3,64]{0,2,1:T(8,128)}, bf16[4,512,3,64]{1,3,2,0:T(8,128)(2,1)}, s32[4]{0:T(128)S(1)}, ...) while((s32[]{:T(128)}, f32[2048,3,64]{0,2,1:T(8,128)S(1)}, ...), condition=%wide.region_15.15_spmd.clone, body=%wide.region_13.14_spmd.clone.sunk | while | flops 2064712704 | bytes 114546992 | solution.py:179
  735.5 7.1 multiply_reduce_fusion.9
  742.6 6.9 multiply_convert_fusion.6
  766.3 7.1 multiply_reduce_fusion.9
  773.5 6.9 multiply_convert_fusion.6
  797.2 7.1 multiply_reduce_fusion.9
  804.3 6.9 multiply_convert_fusion.6
  828.0 7.1 multiply_reduce_fusion.9
  835.2 6.9 multiply_convert_fusion.6
  873.5 11.7 pad_maximum_fusion
  890.6 8.9 convolution_bitcast_fusion
  915.1 9.3 fusion.133
  924.4 36.8 %all-to-all-done.3 = bf16[3,2,2048,192]{3,1,0,2:T(2,128)(2,1)} async-done(((bf16[3,2,2048,192]{3,1,0,2:T(2,128)(2,1)}), bf16[3,2,2048,192]{3,1,0,2:T(2,128)(2,1)}, u32[]{:S(2)}, u32[]{:S(2)}) %all-to-all-start.3) | async-done | bytes 4718624 | tf_op jit(solution)/shard_map/all_to_all | solution.py:271
  961.2 16.2 %copy.237 = bf16[3,2,4,512,192]{3,4,2,1,0:T(8,128)(2,1)} copy(bf16[3,2,4,512,192]{4,1,0,3,2:T(2,128)(2,1)} %bitcast.49) | data formatting | bytes 9437184 | tf_op jit(solution)/shard_map/all_to_all | solution.py:271
  1020.7 8.6 constant_dynamic-update-slice_fusion.5
  1032.4 14.6 %add_convert_fusion = bf16[1024,768]{1,0:T(8,128)(2,1)} fusion(f32[1024,768]{1,0:T(8,128)} %copy-done.6, bf16[96,8,24,128]{3,2,1,0:T(8,128)(2,1)} %bitcast.407, f32[1024,3072]{1,0:T(8,128)} %get-tuple-element.462, f32[3072]{0:T(1024)S(1)} %copy-done.65, f32[768]{0:T(1024)S(1)} %copy-done.67), kind=kOutput, calls=%fused_computation.130 | convolution fusion | flops 4865654784 | bytes 22035456 | tf_op jit(solution)/shard_map/dot_general | solution.py:64
  1049.2 268.4 %reduce-scatter.2.cloned.1.call-done = f32[13,128,128]{2,1,0:T(8,128)} async-done(((f32[416,128,128]{2,1,0:T(8,128)}), f32[13,128,128]{2,1,0:T(8,128)}) %reduce-scatter.2.cloned.1.call-update) | async-done | bytes 851984 | tf_op jit(solution)/shard_map/reduce_scatter | solution.py:314
  1322.8 46.8 %all-reduce = (f32[]{:T(128)}, f32[8832]{0:T(1024)S(1)}) all-reduce(f32[]{:T(128)} %multiply_reduce_fusion.6, f32[8832]{0:T(1024)S(1)} %constant_dynamic-update-slice_fusion.12), channel_id=1, replica_groups=mesh['dp'=8,'seq'=4] {'dp','seq'}, use_global_device_ids=true, to_apply=%region_21.22 | all-reduce | flops 8833 | bytes 70664 | tf_op jit(solution)/shard_map/psum | solution.py:315
  (503 shorter events, 425.4 us)
Async XLA Ops:
  7.2 1365.1 %copy-start = (f32[13,128,128]{2,1,0:T(8,128)S(1)}, f32[13,128,128]{2,1,0:T(8,128)}, u32[]{:S(2)}) copy-start(f32[13,128,128]{2,1,0:T(8,128)} %param.27) | copy-start | bytes 2555908
  7.2 7.3 copy-start.47
  7.2 5.2 copy-start.3
  7.2 107.7 %all-gather.2.cloned.1.call-start = ((), (), s32[]{:S(2)}) async-start(), calls=%async_computation.5 | async-start | bytes 14057472 | tf_op jit(solution)/shard_map/all_gather | solution.py:204
  116.5 8.5 copy-start.22
  121.0 4.7 copy-start.31
  134.1 4.5 copy-start.34
  157.3 59.0 %all-to-all-start = ((bf16[3,2,512,768]{2,1,0,3:T(2,128)(2,1)}), bf16[3,2,512,768]{2,1,0,3:T(2,128)(2,1)}, u32[]{:S(2)}, u32[]{:S(2)}) async-start(bf16[3,2,512,768]{2,1,0,3:T(2,128)(2,1)} %maximum_maximum_fusion), calls=%async_computation | async-start | bytes 9437184 | tf_op jit(solution)/shard_map/all_to_all | solution.py:227
  237.1 5.2 copy-start.71
  445.9 32.1 %all-to-all-start.1 = ((bf16[2,2048,192]{2,0,1:T(2,128)(2,1)}), bf16[2,2048,192]{2,0,1:T(2,128)(2,1)S(1)}, u32[]{:S(2)}, u32[]{:S(2)}) async-start(bf16[2,2048,192]{2,0,1:T(2,128)(2,1)} %copy.225), calls=%async_computation.1 | async-start | bytes 4194304 | tf_op jit(solution)/shard_map/all_to_all | solution.py:231
  479.3 12.4 copy-start.4
  479.3 12.4 copy-start.68
  493.4 45.8 %copy-start.6 = (f32[1024,768]{1,0:T(8,128)}, f32[1024,768]{1,0:T(8,128)S(1)}, u32[]{:S(2)}) copy-start(f32[1024,768]{1,0:T(8,128)S(1)} %get-tuple-element.458) | copy-start | bytes 9437188
  493.5 45.8 %copy-start.43 = (f32[1024]{0:T(1024)}, f32[1024]{0:T(1024)S(1)}, u32[]{:S(2)}) copy-start(f32[1024]{0:T(1024)S(1)} %broadcast_multiply_fusion.6) | copy-start | bytes 12292
  493.5 24.4 %slice-start.5 = ((s8[4718592]{0:T(1024)(128)(4,1)}), s8[4194304]{0:T(1024)(128)(4,1)S(1)}, s32[]{:S(2)}) async-start(s8[4718592]{0:T(1024)(128)(4,1)} %bitcast.408), calls=%async_computation.12 | async-start | bytes 8388608
  494.1 45.2 %copy-start.45 = (f32[1024]{0:T(1024)}, f32[1024]{0:T(1024)S(1)}, u32[]{:S(2)}) copy-start(f32[1024]{0:T(1024)S(1)} %add_rsqrt_fusion) | copy-start | bytes 12292
  495.2 22.7 %copy-start.10 = (bf16[2,512,768]{2,1,0:T(8,128)(2,1)S(1)}, bf16[2,512,768]{2,1,0:T(8,128)(2,1)}, u32[]{:S(2)}) copy-start(bf16[2,512,768]{2,1,0:T(8,128)(2,1)} %get-tuple-element.419) | copy-start | bytes 4718596
  495.2 22.7 %slice-start.6 = ((s8[4718592]{0:T(1024)(128)(4,1)}), s8[524288]{0:T(1024)(128)(4,1)S(1)}, s32[]{:S(2)}) async-start(s8[4718592]{0:T(1024)(128)(4,1)} %bitcast.408), calls=%async_computation.13 | async-start | bytes 1048576
  533.0 6.2 copy-start.14
  544.0 9.3 copy-start.62
  544.0 9.9 copy-start.63
  548.9 24.5 %all-to-all-start.2 = ((bf16[2,512,768]{1,0,2:T(2,128)(2,1)}), bf16[2,512,768]{1,0,2:T(2,128)(2,1)}, u32[]{:S(2)}, u32[]{:S(2)}) async-start(bf16[2,512,768]{1,0,2:T(2,128)(2,1)} %copy.230), calls=%async_computation.2 | async-start | bytes 3145728 | tf_op jit(solution)/shard_map/all_to_all | solution.py:261
  579.7 7.0 copy-start.8
  579.7 7.0 copy-start.41
  579.7 7.0 copy-start.72
  592.4 4.7 copy-start.1
  621.8 6.2 copy-start.1
  652.6 6.2 copy-start.1
  683.5 6.2 copy-start.1
  714.4 3.6 copy-start.9
  714.5 3.6 copy-start.42
  714.5 3.6 copy-start.73
  718.1 7.0 copy-start.8
  718.1 7.0 copy-start.41
  718.1 7.0 copy-start.72
  730.8 4.7 copy-start.1
  760.2 6.2 copy-start.1
  791.0 6.2 copy-start.1
  821.9 6.2 copy-start.1
  852.9 3.6 copy-start.9
  852.9 3.6 copy-start.42
  885.2 5.4 copy-start.44
  885.2 5.4 copy-start.46
  885.2 5.4 copy-start.50
  885.2 5.4 copy-start.52
  885.2 76.0 %all-to-all-start.3 = ((bf16[3,2,2048,192]{3,1,0,2:T(2,128)(2,1)}), bf16[3,2,2048,192]{3,1,0,2:T(2,128)(2,1)}, u32[]{:S(2)}, u32[]{:S(2)}) async-start(bf16[3,2,2048,192]{3,1,0,2:T(2,128)(2,1)} %pad_maximum_fusion), calls=%async_computation.3 | async-start | bytes 12582912 | tf_op jit(solution)/shard_map/all_to_all | solution.py:271
  890.5 427.1 %reduce-scatter.2.cloned.1.call-start = ((), (), s32[]{:S(2)}) async-start(), calls=%async_computation.6 | async-start | bytes 28114944 | tf_op jit(solution)/shard_map/reduce_scatter | solution.py:314
  905.4 9.7 slice-start.3
  909.8 5.3 slice-start.4
  909.8 5.3 copy-start.26
  1010.7 5.8 slice-start
  1010.7 5.8 slice-start.1
  1012.2 4.3 slice-start.2
  1032.4 16.5 %copy-start.70 = (f32[768]{0:T(1024)S(1)}, f32[768]{0:T(1024)}, u32[]{:S(2)}) copy-start(f32[768]{0:T(1024)} %get-tuple-element.333) | copy-start | bytes 9220
  1032.4 16.5 %copy-start.69 = (f32[768]{0:T(1024)S(1)}, f32[768]{0:T(1024)}, u32[]{:S(2)}) copy-start(f32[768]{0:T(1024)} %get-tuple-element.339) | copy-start | bytes 9220
  1032.4 16.5 %copy-start.61 = (f32[768]{0:T(1024)S(1)}, f32[768]{0:T(1024)}, u32[]{:S(2)}) copy-start(f32[768]{0:T(1024)} %get-tuple-element.420) | copy-start | bytes 9220
  1032.4 16.5 %copy-start.60 = (f32[768]{0:T(1024)S(1)}, f32[768]{0:T(1024)}, u32[]{:S(2)}) copy-start(f32[768]{0:T(1024)} %get-tuple-element.418) | copy-start | bytes 9220
  1032.4 16.7 %copy-start.66 = (f32[3072]{0:T(1024)S(1)}, f32[3072]{0:T(1024)}, u32[]{:S(2)}) copy-start(f32[3072]{0:T(1024)} %get-tuple-element.463) | copy-start | bytes 36868
  1047.0 324.5 %copy-start.48 = (f32[8832]{0:T(1024)S(1)}, f32[8832]{0:T(1024)}, u32[]{:S(2)}) copy-start(f32[8832]{0:T(1024)} %param.28) | copy-start | bytes 105988
  1047.0 324.5 %copy-start.55 = (f32[8832]{0:T(1024)S(1)}, f32[8832]{0:T(1024)}, u32[]{:S(2)}) copy-start(f32[8832]{0:T(1024)} %param.29) | copy-start | bytes 105988
  1317.6 54.6 %copy-start.19 = (f32[13,128,128]{2,1,0:T(8,128)S(1)}, f32[13,128,128]{2,1,0:T(8,128)}, u32[]{:S(2)}) copy-start(f32[13,128,128]{2,1,0:T(8,128)} %reduce-scatter.2.cloned.1.call-done) | copy-start | bytes 2555908
  1319.7 54.2 %copy-start.21 = (f32[13,128,128]{1,2,0:T(8,128)S(1)}, f32[13,128,128]{1,2,0:T(8,128)}, u32[]{:S(2)}) copy-start(f32[13,128,128]{1,2,0:T(8,128)} %copy.250) | copy-start | bytes 2555908
  1372.3 9.4 copy-start.7
  1376.9 4.8 copy-start.40
  (49 other events, 107.1 us)
Sparse Core Ops, SparseCore 0:
  11.5 103.4 all-gather.1
  1030.2 287.3 reduce-scatter.1
where the time goes:
time: 1410 us; the launch traced here: 1390 us
  waiting for transfers between devices  465 us (33%)
  matrix products  390 us (28%)
  local copies, waits for them, and re-layouts  260 us (18%)
  other arithmetic  182 us (13%)
  blocking collectives  46.8 us (3%)
  starting transfers between devices  18.8 us (1%)
  between operations  17.8 us (1%)
    reduce_scatter x1, waiting for transfers between devices, per_device(): lax.psum_scatter(grad_stack, ('dp', 'seq'), scatter_dimension=0, tiled=True)  268 us
    all_gather x1, waiting for transfers between devices, per_device(): lax.all_gather(master_tiles.astype(jnp.bfloat16), ('dp', 'seq'), axis=0,...  97.4 us
    dot_general x16, matrix products, one_block(): jnp.einsum('qhd,khd->hqk', query_rows, key_heads, preferred_element_type=...  78.9 us
    dot_general x8, matrix products, one_block(): jnp.einsum('qhd,khd->hqk', grad_rows, value_heads, preferred_element_type...  57.1 us
    convert_element_type x8, other arithmetic, one_block(): score_grad = (probs * (probs_grad - delta)).astype(jnp.bfloat16)  54.9 us
    reduce_sum x8, other arithmetic, one_block(): totals = jnp.sum(exponent, axis=-1, keepdims=True)  54.1 us
    dot_general x8, matrix products, one_block(): jnp.einsum('hqk,khd->qhd', weights, value_heads, preferred_element_type=j...  53.5 us
    all_to_all x1, waiting for transfers between devices, per_device(): lax.all_to_all(packed, 'seq', split_axis=3, concat_axis=2, tiled=True)  53.2 us
  transfers between devices with their start and end apart: 6, of which 5 were waited for; matrix products, arithmetic and copies ran while one was open for 7% of the time, Pallas kernels for 0%

commit v1 on v0

--- a/solution.py
+++ b/solution.py
@@ -268,12 +268,18 @@
     query_grad, key_grad, value_grad = lax.map(
         attend_backward, (head_data[0], head_data[1], head_data[2], grad_heads, log_sums, lengths)
     )
-    sent_back = lax.all_to_all(
-        jnp.stack([query_grad, key_grad, value_grad]),
-        "seq",
-        split_axis=2,
-        concat_axis=3,
-        tiled=True,
+    sent_back = jnp.concatenate(
+        lax.all_to_all(
+            jnp.stack(
+                jnp.split(
+                    jnp.stack([query_grad, key_grad, value_grad]), lax.axis_size("seq"), axis=2
+                )
+            ),
+            "seq",
+            0,
+            0,
+        ),
+        axis=3,
     )
     queries_grad = sent_back[0].reshape(-1, model_width)
     keys_grad = sent_back[1].reshape(-1, model_width)

time: 1410 us -> 1340 us (0.950)
  local copies, waits for them, and re-layouts: 260 us -> 228 us
  waiting for transfers between devices: 465 us -> 447 us
    all_to_all x1, waiting for transfers between devices: 36.8 us -> 19.8 us  [per_device(): lax.all_to_all(jnp.stack(jnp.split(jnp.stack([query_grad, key_grad, value...]
    while x75 -> x72, local copies, waits for them, and re-layouts: 20.2 us -> 3.5 us  [the longest x3 16.8 us: per_device(): lax.map(attend_backward, (head_data[0], head_data[1], head_data[2], grad_...]
    all_to_all x1 -> x0, local copies, waits for them, and re-layouts: 16.2 us -> none  [per_device(): lax.all_to_all(jnp.stack([query_grad, key_grad, value_grad]), 'seq', spli...]
where the time goes in v1:
time: 1340 us; the launch traced here: 1330 us
  waiting for transfers between devices  447 us (33%)
  matrix products  382 us (29%)
  local copies, waits for them, and re-layouts  228 us (17%)
  other arithmetic  176 us (13%)
  blocking collectives  46.8 us (3%)
  starting transfers between devices  18.4 us (1%)
  between operations  18 us (1%)
    reduce_scatter x1, waiting for transfers between devices, per_device(): lax.psum_scatter(grad_stack, ('dp', 'seq'), scatter_dimension=0, tiled=True)  268 us
    all_gather x1, waiting for transfers between devices, per_device(): lax.all_gather(master_tiles.astype(jnp.bfloat16), ('dp', 'seq'), axis=0,...  97.4 us
    dot_general x16, matrix products, one_block(): jnp.einsum('qhd,khd->hqk', query_rows, key_heads, preferred_element_type=...  80.5 us
    dot_general x8, matrix products, one_block(): jnp.einsum('qhd,khd->hqk', grad_rows, value_heads, preferred_element_type...  57.8 us
    convert_element_type x8, other arithmetic, one_block(): score_grad = (probs * (probs_grad - delta)).astype(jnp.bfloat16)  54.9 us
    reduce_sum x8, other arithmetic, one_block(): totals = jnp.sum(exponent, axis=-1, keepdims=True)  54.1 us
    dot_general x8, matrix products, one_block(): jnp.einsum('hqk,khd->qhd', weights, value_heads, preferred_element_type=j...  53.5 us
    all_to_all x1, waiting for transfers between devices, per_device(): lax.all_to_all(packed, 'seq', split_axis=3, concat_axis=2, tiled=True)  53.2 us
  transfers between devices with their start and end apart: 6, of which 5 were waited for; matrix products, arithmetic and copies ran while one was open for 7% of the time, Pallas kernels for 0%

profile of v1, /device:TPU:0, one launch (start us, length us, event | category | flops | bytes accessed | tf_op | source)
XLA Modules:
  0.0 1329.2 jit_solution(3531026092134601013)
XLA Ops:
  17.5 97.4 %all-gather.2.cloned.1.call-done = bf16[416,128,128]{2,1,0:T(8,128)(2,1)} async-done(((bf16[13,128,128]{2,1,0:T(8,128)(2,1)}), bf16[416,128,128]{2,1,0:T(8,128)(2,1)}) %all-gather.2.cloned.1.call-update) | async-done | bytes 13631504 | tf_op jit(solution)/shard_map/all_gather | solution.py:204
  143.5 13.8 %maximum_maximum_fusion = bf16[3,2,512,768]{2,1,0,3:T(2,128)(2,1)} fusion(bf16[1,2,512,384]{2,1,0,3:T(2,128)(2,1)S(1)} %bitcast.423, bf16[1,2,512,384]{2,1,0,3:T(2,128)(2,1)} %copy.104, bf16[1,2,512,768]{2,1,0,3:T(2,128)(2,1)S(1)} %copy.106, bf16[1,2,512,768]{2,1,0,3:T(2,128)(2,1)} %copy.105), kind=kLoop, calls=%fused_computation.93 | loop fusion | flops 7077888 | bytes 9437184 | tf_op jit(solution)/shard_map/stack | solution.py:224
  163.2 53.2 %all-to-all-done = bf16[3,2,512,768]{2,1,0,3:T(2,128)(2,1)} async-done(((bf16[3,2,512,768]{2,1,0,3:T(2,128)(2,1)}), bf16[3,2,512,768]{2,1,0,3:T(2,128)(2,1)}, u32[]{:S(2)}, u32[]{:S(2)}) %all-to-all-start) | async-done | bytes 4718624 | tf_op jit(solution)/shard_map/all_to_all | solution.py:227
  242.4 199.3 %while.54 = (s32[]{:T(128)}, bf16[2,2048,192]{1,2,0:T(8,128)(2,1)}, f32[2,3,2048]{2,1,0:T(4,128)S(1)}, bf16[2,2048,192]{1,2,0:T(8,128)(2,1)}, bf16[2,2048,192]{1...) while((s32[]{:T(128)}, bf16[2,2048,192]{1,2,0:T(8,128)(2,1)}, ...), condition=%wide.region_7.8_spmd, body=%wide.region_2.7_spmd.sunk | while | flops 845251584 | bytes 53479908 | solution.py:228
  247.1 93.0 %while.57 = (s32[]{:T(128)}, bf16[4,512,3,64]{1,3,2,0:T(8,128)(2,1)S(1)}, f32[4,3,512]{2,1,0:T(4,128)S(1)}, s32[4]{0:T(128)S(1)}, s32[]{:T(128)}, /*index=5*/bf1...) while((s32[]{:T(128)}, ...), condition=%wide.region_6.6_spmd, body=%wide.region_3.5_spmd.sunk | while | flops 845251584 | bytes 43976908 | solution.py:128
  249.6 7.2 fusion.206
  256.9 6.8 fusion.207
  263.6 6.7 fusion.208
  272.9 7.2 fusion.206
  280.1 6.8 fusion.207
  286.9 6.7 fusion.208
  296.1 7.2 fusion.206
  303.4 6.8 fusion.207
  310.1 6.7 fusion.208
  319.4 7.2 fusion.206
  326.6 6.8 fusion.207
  333.4 6.7 fusion.208
  346.5 93.0 %while.57 = (s32[]{:T(128)}, bf16[4,512,3,64]{1,3,2,0:T(8,128)(2,1)S(1)}, f32[4,3,512]{2,1,0:T(4,128)S(1)}, s32[4]{0:T(128)S(1)}, s32[]{:T(128)}, /*index=5*/bf1...) while((s32[]{:T(128)}, ...), condition=%wide.region_6.6_spmd, body=%wide.region_3.5_spmd.sunk | while | flops 845251584 | bytes 43976908 | solution.py:128
  349.0 7.2 fusion.206
  356.2 6.8 fusion.207
  363.0 6.7 fusion.208
  372.3 7.2 fusion.206
  379.5 6.8 fusion.207
  386.3 6.7 fusion.208
  395.5 7.2 fusion.206
  402.8 6.8 fusion.207
  409.5 6.7 fusion.208
  418.8 7.2 fusion.206
  426.0 6.8 fusion.207
  432.8 6.7 fusion.208
  455.2 9.1 fusion.122
  469.5 6.9 copy.115
  481.0 10.4 copy.112
  496.9 12.5 fusion.54
  509.4 15.1 %convert_reduce_fusion = (f32[3072]{0:T(1024)}, bf16[1024,3072]{1,0:T(8,128)(2,1)S(1)}) fusion(f32[1024,3072]{1,0:T(8,128)} %get-tuple-element.433, f32[3072]{0:T(1024)S(1)} %copy-done.64, bf16[1024,768]{1,0:T(8,128)(2,1)S(1)} %bitcast.396, bf16[96,8,24,128]{3,2,1,0:T(8,128)(2,1)S(1)} %bitcast.415), kind=kOutput, calls=%fused_computation.82 | convolution fusion | flops 4904186880 | bytes 25190400 | tf_op jit(solution)/shard_map/dot_general | solution.py:74
  524.5 6.2 multiply_reduce_fusion.1
  547.6 8.7 copy.138
  556.3 8.6 all-to-all-done.2
  570.9 278.0 %while.56 = (s32[]{:T(128)}, bf16[2,2048,192]{1,2,0:T(8,128)(2,1)}, bf16[2,2048,192]{1,2,0:T(8,128)(2,1)}, bf16[2,2048,192]{1,2,0:T(8,128)(2,1)}, bf16[2,2048,19...) while((s32[]{:T(128)}, bf16[2,2048,192]{1,2,0:T(8,128)(2,1)}, ...), condition=%wide.region_16.17_spmd, body=%wide.region_12.16_spmd.sunk | while | flops 2065499136 | bytes 171613168 | solution.py:268
  578.2 122.2 %while.58 = (s32[]{:T(128)}, f32[2048,3,64]{0,2,1:T(8,128)S(1)}, f32[2048,3,64]{0,2,1:T(8,128)}, bf16[4,512,3,64]{1,3,2,0:T(8,128)(2,1)}, s32[4]{0:T(128)S(1)}, ...) while((s32[]{:T(128)}, f32[2048,3,64]{0,2,1:T(8,128)S(1)}, ...), condition=%wide.region_15.15_spmd.clone, body=%wide.region_13.14_spmd.clone.sunk | while | flops 2064712704 | bytes 114546992 | solution.py:179
  588.5 7.2 multiply_reduce_fusion.9
  595.7 6.9 multiply_convert_fusion.6
  619.4 7.2 multiply_reduce_fusion.9
  626.6 6.9 multiply_convert_fusion.6
  650.3 7.2 multiply_reduce_fusion.9
  657.6 6.9 multiply_convert_fusion.6
  681.2 7.2 multiply_reduce_fusion.9
  688.4 6.9 multiply_convert_fusion.6
  716.9 122.1 %while.58 = (s32[]{:T(128)}, f32[2048,3,64]{0,2,1:T(8,128)S(1)}, f32[2048,3,64]{0,2,1:T(8,128)}, bf16[4,512,3,64]{1,3,2,0:T(8,128)(2,1)}, s32[4]{0:T(128)S(1)}, ...) while((s32[]{:T(128)}, f32[2048,3,64]{0,2,1:T(8,128)S(1)}, ...), condition=%wide.region_15.15_spmd.clone, body=%wide.region_13.14_spmd.clone.sunk | while | flops 2064712704 | bytes 114546992 | solution.py:179
  727.2 7.2 multiply_reduce_fusion.9
  734.5 6.9 multiply_convert_fusion.6
  758.1 7.2 multiply_reduce_fusion.9
  765.4 6.9 multiply_convert_fusion.6
  789.0 7.2 multiply_reduce_fusion.9
  796.3 6.9 multiply_convert_fusion.6
  820.0 7.2 multiply_reduce_fusion.9
  827.2 6.9 multiply_convert_fusion.6
  859.6 8.9 convolution_bitcast_fusion
  884.1 9.5 fusion.133
  893.6 19.8 %all-to-all-done.3 = bf16[4,3,2,512,192]{3,4,2,1,0:T(8,128)(2,1)} async-done(((bf16[4,3,2,512,192]{3,4,2,1,0:T(8,128)(2,1)}), bf16[4,3,2,512,192]{3,4,2,1,0:T(8,128)(2,1)}, u32[]{:S(2)}, u32[]{:S(2)}) %all-to-all-start.3) | async-done | bytes 4718624 | tf_op jit(solution)/shard_map/all_to_all | solution.py:272
  956.9 8.8 constant_dynamic-update-slice_fusion.5
  968.8 14.6 %add_convert_fusion = bf16[1024,768]{1,0:T(8,128)(2,1)} fusion(f32[1024,768]{1,0:T(8,128)} %copy-done.6, bf16[96,8,24,128]{3,2,1,0:T(8,128)(2,1)} %bitcast.412, f32[1024,3072]{1,0:T(8,128)} %get-tuple-element.433, f32[3072]{0:T(1024)S(1)} %copy-done.65, f32[768]{0:T(1024)S(1)} %copy-done.67), kind=kOutput, calls=%fused_computation.131 | convolution fusion | flops 4865654784 | bytes 22035456 | tf_op jit(solution)/shard_map/dot_general | solution.py:64
  985.5 268.4 %reduce-scatter.2.cloned.1.call-done = f32[13,128,128]{2,1,0:T(8,128)} async-done(((f32[416,128,128]{2,1,0:T(8,128)}), f32[13,128,128]{2,1,0:T(8,128)}) %reduce-scatter.2.cloned.1.call-update) | async-done | bytes 851984 | tf_op jit(solution)/shard_map/reduce_scatter | solution.py:320
  1259.1 46.8 %all-reduce = (f32[]{:T(128)}, f32[8832]{0:T(1024)S(1)}) all-reduce(f32[]{:T(128)} %multiply_reduce_fusion.6, f32[8832]{0:T(1024)S(1)} %constant_dynamic-update-slice_fusion.12), channel_id=1, replica_groups=mesh['dp'=8,'seq'=4] {'dp','seq'}, use_global_device_ids=true, to_apply=%region_21.22 | all-reduce | flops 8833 | bytes 70664 | tf_op jit(solution)/shard_map/psum | solution.py:321
  (501 shorter events, 401.7 us)
Async XLA Ops:
  7.2 1301.4 %copy-start = (f32[13,128,128]{2,1,0:T(8,128)S(1)}, f32[13,128,128]{2,1,0:T(8,128)}, u32[]{:S(2)}) copy-start(f32[13,128,128]{2,1,0:T(8,128)} %param.27) | copy-start | bytes 2555908
  7.2 7.3 copy-start.47
  7.2 5.2 copy-start.3
  7.2 107.7 %all-gather.2.cloned.1.call-start = ((), (), s32[]{:S(2)}) async-start(), calls=%async_computation.5 | async-start | bytes 14057472 | tf_op jit(solution)/shard_map/all_gather | solution.py:204
  116.5 8.5 copy-start.22
  121.0 4.7 copy-start.31
  134.1 4.5 copy-start.34
  157.3 59.1 %all-to-all-start = ((bf16[3,2,512,768]{2,1,0,3:T(2,128)(2,1)}), bf16[3,2,512,768]{2,1,0,3:T(2,128)(2,1)}, u32[]{:S(2)}, u32[]{:S(2)}) async-start(bf16[3,2,512,768]{2,1,0,3:T(2,128)(2,1)} %maximum_maximum_fusion), calls=%async_computation | async-start | bytes 9437184 | tf_op jit(solution)/shard_map/all_to_all | solution.py:227
  237.2 5.2 copy-start.71
  447.7 32.0 %all-to-all-start.1 = ((bf16[2,2048,192]{2,0,1:T(2,128)(2,1)}), bf16[2,2048,192]{2,0,1:T(2,128)(2,1)S(1)}, u32[]{:S(2)}, u32[]{:S(2)}) async-start(bf16[2,2048,192]{2,0,1:T(2,128)(2,1)} %copy.111), calls=%async_computation.1 | async-start | bytes 4194304 | tf_op jit(solution)/shard_map/all_to_all | solution.py:231
  481.0 12.4 copy-start.4
  481.0 12.4 copy-start.68
  495.2 35.6 %copy-start.6 = (f32[1024,768]{1,0:T(8,128)}, f32[1024,768]{1,0:T(8,128)S(1)}, u32[]{:S(2)}) copy-start(f32[1024,768]{1,0:T(8,128)S(1)} %get-tuple-element.429) | copy-start | bytes 9437188
  495.2 35.5 %copy-start.43 = (f32[1024]{0:T(1024)}, f32[1024]{0:T(1024)S(1)}, u32[]{:S(2)}) copy-start(f32[1024]{0:T(1024)S(1)} %broadcast_multiply_fusion.6) | copy-start | bytes 12292
  495.2 14.1 %slice-start.5 = ((s8[4718592]{0:T(1024)(128)(4,1)}), s8[4194304]{0:T(1024)(128)(4,1)S(1)}, s32[]{:S(2)}) async-start(s8[4718592]{0:T(1024)(128)(4,1)} %bitcast.413), calls=%async_computation.12 | async-start | bytes 8388608
  495.8 35.0 %copy-start.45 = (f32[1024]{0:T(1024)}, f32[1024]{0:T(1024)S(1)}, u32[]{:S(2)}) copy-start(f32[1024]{0:T(1024)S(1)} %add_rsqrt_fusion) | copy-start | bytes 12292
  496.9 12.5 copy-start.10
  496.9 12.5 slice-start.6
  524.5 6.2 copy-start.14
  535.5 9.3 copy-start.62
  535.5 9.9 copy-start.63
  540.4 24.5 %all-to-all-start.2 = ((bf16[2,512,768]{1,0,2:T(2,128)(2,1)}), bf16[2,512,768]{1,0,2:T(2,128)(2,1)}, u32[]{:S(2)}, u32[]{:S(2)}) async-start(bf16[2,512,768]{1,0,2:T(2,128)(2,1)} %copy.116), calls=%async_computation.2 | async-start | bytes 3145728 | tf_op jit(solution)/shard_map/all_to_all | solution.py:261
  571.0 7.1 copy-start.8
  571.1 7.1 copy-start.41
  571.1 7.1 copy-start.72
  583.8 4.7 copy-start.1
  613.2 6.2 copy-start.1
  644.1 6.2 copy-start.1
  675.1 6.2 copy-start.1
  706.1 3.6 copy-start.9
  706.1 3.6 copy-start.42
  706.2 3.6 copy-start.73
  709.8 7.1 copy-start.8
  709.8 7.1 copy-start.41
  709.8 7.1 copy-start.72
  722.5 4.7 copy-start.1
  752.0 6.2 copy-start.1
  782.9 6.2 copy-start.1
  813.8 6.2 copy-start.1
  844.9 3.6 copy-start.9
  844.9 3.6 copy-start.42
  854.6 5.0 copy-start.44
  854.6 5.0 copy-start.46
  854.6 5.0 copy-start.50
  854.6 5.1 copy-start.52
  854.6 58.8 %all-to-all-start.3 = ((bf16[4,3,2,512,192]{3,4,2,1,0:T(8,128)(2,1)}), bf16[4,3,2,512,192]{3,4,2,1,0:T(8,128)(2,1)}, u32[]{:S(2)}, u32[]{:S(2)}) async-start(bf16[4,3,2,512,192]{3,4,2,1,0:T(8,128)(2,1)} %pad_maximum_fusion.1), calls=%async_computation.3 | async-start | bytes 9437184 | tf_op jit(solution)/shard_map/all_to_all | solution.py:272
  859.5 394.4 %reduce-scatter.2.cloned.1.call-start = ((), (), s32[]{:S(2)}) async-start(), calls=%async_computation.6 | async-start | bytes 28114944 | tf_op jit(solution)/shard_map/reduce_scatter | solution.py:320
  874.4 9.7 slice-start.3
  878.9 5.2 slice-start.4
  878.9 5.2 copy-start.26
  946.7 5.8 slice-start
  946.7 5.8 slice-start.1
  948.2 4.4 slice-start.2
  968.7 16.5 %copy-start.70 = (f32[768]{0:T(1024)S(1)}, f32[768]{0:T(1024)}, u32[]{:S(2)}) copy-start(f32[768]{0:T(1024)} %get-tuple-element.300) | copy-start | bytes 9220
  968.7 16.5 %copy-start.69 = (f32[768]{0:T(1024)S(1)}, f32[768]{0:T(1024)}, u32[]{:S(2)}) copy-start(f32[768]{0:T(1024)} %get-tuple-element.306) | copy-start | bytes 9220
  968.7 16.6 %copy-start.61 = (f32[768]{0:T(1024)S(1)}, f32[768]{0:T(1024)}, u32[]{:S(2)}) copy-start(f32[768]{0:T(1024)} %get-tuple-element.387) | copy-start | bytes 9220
  968.7 16.6 %copy-start.60 = (f32[768]{0:T(1024)S(1)}, f32[768]{0:T(1024)}, u32[]{:S(2)}) copy-start(f32[768]{0:T(1024)} %get-tuple-element.385) | copy-start | bytes 9220
  968.7 16.8 %copy-start.66 = (f32[3072]{0:T(1024)S(1)}, f32[3072]{0:T(1024)}, u32[]{:S(2)}) copy-start(f32[3072]{0:T(1024)} %get-tuple-element.434) | copy-start | bytes 36868
  983.4 324.5 %copy-start.48 = (f32[8832]{0:T(1024)S(1)}, f32[8832]{0:T(1024)}, u32[]{:S(2)}) copy-start(f32[8832]{0:T(1024)} %param.28) | copy-start | bytes 105988
  983.4 324.5 %copy-start.55 = (f32[8832]{0:T(1024)S(1)}, f32[8832]{0:T(1024)}, u32[]{:S(2)}) copy-start(f32[8832]{0:T(1024)} %param.29) | copy-start | bytes 105988
  1253.9 54.6 %copy-start.19 = (f32[13,128,128]{2,1,0:T(8,128)S(1)}, f32[13,128,128]{2,1,0:T(8,128)}, u32[]{:S(2)}) copy-start(f32[13,128,128]{2,1,0:T(8,128)} %reduce-scatter.2.cloned.1.call-done) | copy-start | bytes 2555908
  1256.0 54.2 %copy-start.21 = (f32[13,128,128]{1,2,0:T(8,128)S(1)}, f32[13,128,128]{1,2,0:T(8,128)}, u32[]{:S(2)}) copy-start(f32[13,128,128]{1,2,0:T(8,128)} %copy.129) | copy-start | bytes 2555908
  1308.6 9.4 copy-start.7
  1313.2 4.8 copy-start.40
  (49 other events, 107.3 us)
Sparse Core Ops, SparseCore 0:
  11.5 103.4 all-gather.1
  966.5 287.3 reduce-scatter.1
